TPU v7x, 128 devices: a whole 4x4x4 slice. The times are simulated.
128 devices in a mesh: ctx: 32 (over x, y_lo, z), exp: 4 (over y_hi, core).
Axes of the slice: x: 4, y: 4 (y_hi: 2, y_lo: 2; y = y_hi * 2 + y_lo), z: 4, core: 2. Of those that a mesh axis runs over, the one named last changes fastest.
Arguments:
- residual: bfloat16 [4, 4096, 2048], P('exp', 'ctx'), may hold values from -6 to 6
- query_heads: bfloat16 [4, 4096, 2048], P('exp', 'ctx'), may hold values from -6.5 to 6.5
- key_heads: bfloat16 [4, 4096, 256], P('exp', 'ctx'), may hold values from -6 to 6
- value_heads: bfloat16 [4, 4096, 256], P('exp', 'ctx'), may hold values from -6 to 6
- norm_gain: float32 [2048], replicated, may hold values from 0.1 to 1.9
- chosen_experts: int32 [4, 4096, 8], P('exp', 'ctx'), may hold values from 0 to 127, all different within a row; in each aligned block of 128 rows (0 to 127, 128 to 255, ..., all dimensions but the last counted through in order) at most 9 rows name the same one
- route_weights: float32 [4, 4096, 8], P('exp', 'ctx'), may hold values from 0.05 to 1
- gate_weight: bfloat16 [128, 2048, 768], P(('ctx', 'exp')), may hold values from -0.125 to 0.125
- up_weight: bfloat16 [128, 2048, 768], P(('ctx', 'exp')), may hold values from -0.125 to 0.125
- down_weight: bfloat16 [128, 768, 2048], P(('ctx', 'exp')), may hold values from -0.21875 to 0.21875
- cotangent: bfloat16 [4, 4096, 2048], P('exp', 'ctx'), may hold values from -6 to 6
Outputs:
- layer_out: bfloat16 [4, 4096, 2048], P('exp', 'ctx')
- residual_gradient: bfloat16 [4, 4096, 2048], P('exp', 'ctx')
- query_gradient: bfloat16 [4, 4096, 2048], P('exp', 'ctx')
- key_gradient: bfloat16 [4, 4096, 256], P('exp', 'ctx')
- value_gradient: bfloat16 [4, 4096, 256], P('exp', 'ctx')
- route_gradient: float32 [4, 4096, 8], P('exp', 'ctx')
Inputs may be any that keep to these rules, and one draw needn't show every extreme that they name: `chosen_experts`: among the rows of one device no expert is named by more than 9 rows, a bound that some block reaches; the 8 experts of a row differ.
All inputs are finite; a program needn't handle non-finite values.
Results may differ from a plain program's by a relative error of at most 0.025.
Values may be sent and summed in bfloat16 or wider, within the bound.
A program may use at most 192 MiB of HBM per device.

v0:
```python
import jax
import jax.numpy as jnp
from jax import lax
from jax.sharding import PartitionSpec as P

H = 16
KVH = 2
DH = 128
TOPK = 8
NEG = -1e30
EPSILON = 1e-06


def place_rows(begin_row, row_count):
    row_index = begin_row + jnp.arange(row_count, dtype=jnp.int32)
    return row_index


def over_keys(key_local, value_local, visit, start_state):
    return visit(
        start_state,
        (
            lax.all_gather(key_local, "ctx", axis=0, tiled=True),
            lax.all_gather(value_local, "ctx", axis=0, tiled=True),
        ),
        jnp.int32(0),
    )


def to_experts(rows_out):
    return lax.all_to_all(rows_out, ("ctx", "exp"), split_axis=0, concat_axis=0, tiled=True)


def from_experts(rows_back):
    return lax.all_to_all(rows_back, ("ctx", "exp"), split_axis=0, concat_axis=0, tiled=True)


def forward_tile(state, query_half, query_place, key_block, value_block, key_place, score_scale):
    run_max, run_sum, run_acc = state
    scores = (
        jnp.einsum("ikgd,jkd->kgij", query_half, key_block, preferred_element_type=jnp.float32)
        * score_scale
    )
    allowed = key_place[None, :] <= query_place[:, None]
    scores = jnp.where(allowed, scores, NEG)
    new_max = jnp.maximum(run_max, jnp.max(scores, axis=-1))
    weights = jnp.where(allowed, jnp.exp(scores - new_max[..., None]), 0.0)
    run_sum = jnp.sum(weights, axis=-1)
    run_acc = jnp.einsum(
        "kgij,jkd->kgid",
        weights.astype(jnp.bfloat16),
        value_block,
        preferred_element_type=jnp.float32,
    )
    return (new_max, run_sum, run_acc)


def backward_tile(
    query_acc,
    query_half,
    query_place,
    grad_half,
    log_half,
    dot_half,
    key_block,
    value_block,
    key_place,
    score_scale,
):
    scores = (
        jnp.einsum("ikgd,jkd->kgij", query_half, key_block, preferred_element_type=jnp.float32)
        * score_scale
    )
    allowed = key_place[None, :] <= query_place[:, None]
    weights = jnp.where(allowed, jnp.exp(scores - log_half[..., None]), 0.0)
    value_part = jnp.einsum(
        "kgij,ikgd->jkd",
        weights.astype(jnp.bfloat16),
        grad_half,
        preferred_element_type=jnp.float32,
    )
    grad_weights = jnp.einsum(
        "ikgd,jkd->kgij", grad_half, value_block, preferred_element_type=jnp.float32
    )
    grad_scores = (weights * (grad_weights - dot_half[..., None])).astype(jnp.bfloat16)
    query_acc = (
        jnp.einsum("kgij,jkd->kgid", grad_scores, key_block, preferred_element_type=jnp.float32)
        * score_scale
    )
    key_part = (
        jnp.einsum("kgij,ikgd->jkd", grad_scores, query_half, preferred_element_type=jnp.float32)
        * score_scale
    )
    return (query_acc, key_part, value_part)


def per_device(
    residual,
    query_heads,
    key_heads,
    value_heads,
    norm_gain,
    chosen_experts,
    route_weights,
    gate_weight,
    up_weight,
    down_weight,
    cotangent,
):
    shard_rows = residual.shape[1]
    width = residual.shape[2]
    kv_width = key_heads.shape[2]
    query_width = query_heads.shape[2]
    group_size = H // KVH
    half_rows = shard_rows // 2
    ctx_count = lax.axis_size("ctx")
    seq_rows = shard_rows * ctx_count
    score_scale = DH ** (-0.5)
    ctx_index = lax.axis_index("ctx")
    packed = jnp.concatenate([query_heads[0], key_heads[0], value_heads[0]], axis=1)
    query_local = packed[:, :query_width].reshape(shard_rows, KVH, group_size, DH)
    key_local = packed[:, query_width : query_width + kv_width]
    value_local = packed[:, query_width + kv_width :]
    query_place = place_rows(ctx_index * shard_rows, shard_rows)

    def forward_visit(state, piece, begin_row):
        key_rows, value_rows = piece
        row_count = key_rows.shape[0]
        key_block = key_rows.reshape(row_count, KVH, DH)
        value_block = value_rows.reshape(row_count, KVH, DH)
        key_place = place_rows(begin_row, row_count)
        updated = []
        for which_half in range(2):
            query_half = query_local[which_half * half_rows : (which_half + 1) * half_rows]
            place_half = query_place[which_half * half_rows : (which_half + 1) * half_rows]
            updated.append(
                lax.cond(
                    jnp.min(key_place) <= jnp.max(place_half),
                    lambda inner: forward_tile(
                        inner,
                        query_half,
                        place_half,
                        key_block,
                        value_block,
                        key_place,
                        score_scale,
                    ),
                    lambda inner: inner,
                    state[which_half],
                )
            )
        return tuple(updated)

    start_half = (
        jnp.full((KVH, group_size, half_rows), NEG, jnp.float32),
        jnp.zeros((KVH, group_size, half_rows), jnp.float32),
        jnp.zeros((KVH, group_size, half_rows, DH), jnp.float32),
    )
    halves = over_keys(key_local, value_local, forward_visit, (start_half, start_half))
    attended = jnp.concatenate(
        [acc_half / sum_half[..., None] for max_half, sum_half, acc_half in halves], axis=2
    )
    log_sum = jnp.concatenate(
        [max_half + jnp.log(sum_half) for max_half, sum_half, acc_half in halves], axis=2
    )
    attended_local = (
        jnp.transpose(attended, (2, 0, 1, 3)).reshape(shard_rows, query_width).astype(jnp.bfloat16)
    )
    hidden = (residual[0].astype(jnp.float32) + attended_local.astype(jnp.float32)).astype(
        jnp.bfloat16
    )
    hidden_float = hidden.astype(jnp.float32)
    inverse = lax.rsqrt(jnp.mean(hidden_float * hidden_float, axis=-1, keepdims=True) + EPSILON)
    normed = (hidden_float * inverse * norm_gain).astype(jnp.bfloat16)
    expert_count = ctx_count * lax.axis_size("exp")
    capacity = (9 * shard_rows * TOPK + 8 * expert_count - 1) // (8 * expert_count)
    chosen_flat = chosen_experts[0].reshape(-1)
    onehot_hits = (
        chosen_flat[:, None] == jnp.arange(expert_count, dtype=jnp.int32)[None, :]
    ).astype(jnp.int32)
    earlier = jnp.cumsum(onehot_hits, axis=0) - onehot_hits
    slot_index = jnp.sum(earlier * onehot_hits, axis=1)
    target = chosen_flat * capacity + slot_index
    share_raw = route_weights[0]
    route_total = jnp.sum(share_raw, axis=-1, keepdims=True)
    route_share = share_raw / route_total
    cot_float = cotangent[0].astype(jnp.float32)

    def spread(row_values):
        filled = (
            jnp.zeros((expert_count * capacity, width), jnp.bfloat16).at[target].set(row_values)
        )
        return filled.reshape(expert_count, capacity, width)

    gate_mat = gate_weight[0]
    up_mat = up_weight[0]
    down_mat = down_weight[0]
    incoming = to_experts(spread(jnp.repeat(normed, TOPK, axis=0))).reshape(-1, width)
    gate_act = jnp.dot(incoming, gate_mat, preferred_element_type=jnp.float32)
    up_act = jnp.dot(incoming, up_mat, preferred_element_type=jnp.float32)
    activation = (jax.nn.silu(gate_act) * up_act).astype(jnp.bfloat16)
    produced = jnp.dot(activation, down_mat, preferred_element_type=jnp.float32).astype(
        jnp.bfloat16
    )
    returned = from_experts(produced.reshape(expert_count, capacity, width)).reshape(-1, width)
    picked = returned[target].reshape(shard_rows, TOPK, width)
    moe_sum = jnp.sum(route_share[:, :, None] * picked.astype(jnp.float32), axis=1)
    layer_out = (hidden_float + moe_sum).astype(jnp.bfloat16)
    route_dot = jnp.sum(picked.astype(jnp.float32) * cot_float[:, None, :], axis=-1)
    route_gradient = (
        route_dot - jnp.sum(route_share * route_dot, axis=-1, keepdims=True)
    ) / route_total
    out_cot = (
        (route_share[:, :, None] * cot_float[:, None, :]).astype(jnp.bfloat16).reshape(-1, width)
    )
    cot_in = to_experts(spread(out_cot)).reshape(-1, width)
    act_cot = lax.dot_general(
        cot_in, down_mat, (((1,), (1,)), ((), ())), preferred_element_type=jnp.float32
    )
    sigma_gate = jax.nn.sigmoid(gate_act)
    gate_cot = (act_cot * up_act * sigma_gate * (1.0 + gate_act * (1.0 - sigma_gate))).astype(
        jnp.bfloat16
    )
    up_cot = (act_cot * gate_act * sigma_gate).astype(jnp.bfloat16)
    row_cot = (
        lax.dot_general(
            gate_cot, gate_mat, (((1,), (1,)), ((), ())), preferred_element_type=jnp.float32
        )
        + lax.dot_general(
            up_cot, up_mat, (((1,), (1,)), ((), ())), preferred_element_type=jnp.float32
        )
    ).astype(jnp.bfloat16)
    cot_back = from_experts(row_cot.reshape(expert_count, capacity, width)).reshape(-1, width)
    normed_cot = jnp.sum(
        cot_back[target].reshape(shard_rows, TOPK, width).astype(jnp.float32), axis=1
    )
    gained = norm_gain * normed_cot
    hidden_cot = inverse * gained - hidden_float * inverse**3 * jnp.mean(
        hidden_float * gained, axis=-1, keepdims=True
    )
    residual_gradient = (cot_float + hidden_cot).astype(jnp.bfloat16)
    grad_local = residual_gradient.reshape(shard_rows, KVH, group_size, DH)
    attended_rows = attended_local.reshape(shard_rows, KVH, group_size, DH)
    row_dot = jnp.einsum(
        "ikgd,ikgd->kgi", grad_local, attended_rows, preferred_element_type=jnp.float32
    )

    def backward_visit(state, piece, begin_row):
        query_accs, key_total, value_total = state
        key_rows, value_rows = piece
        row_count = key_rows.shape[0]
        key_block = key_rows.reshape(row_count, KVH, DH)
        value_block = value_rows.reshape(row_count, KVH, DH)
        key_place = place_rows(begin_row, row_count)
        empty_block = jnp.zeros((row_count, KVH, DH), jnp.float32)
        key_sum = empty_block
        value_sum = empty_block
        new_accs = []
        for which_half in range(2):
            lower = which_half * half_rows
            upper = lower + half_rows
            query_half = query_local[lower:upper]
            place_half = query_place[lower:upper]
            grad_half = grad_local[lower:upper]
            log_half = log_sum[:, :, lower:upper]
            dot_half = row_dot[:, :, lower:upper]
            query_acc, key_part, value_part = lax.cond(
                jnp.min(key_place) <= jnp.max(place_half),
                lambda inner: backward_tile(
                    inner,
                    query_half,
                    place_half,
                    grad_half,
                    log_half,
                    dot_half,
                    key_block,
                    value_block,
                    key_place,
                    score_scale,
                ),
                lambda inner: (inner, empty_block, empty_block),
                query_accs[which_half],
            )
            new_accs.append(query_acc)
            key_sum = key_sum + key_part
            value_sum = value_sum + value_part
        key_total = key_sum.reshape(row_count, -1)
        value_total = value_sum.reshape(row_count, -1)
        return (tuple(new_accs), key_total, value_total)

    empty_query = jnp.zeros((KVH, group_size, half_rows, DH), jnp.float32)
    empty_keys = jnp.zeros((seq_rows, kv_width), jnp.float32)
    query_accs, key_total, value_total = over_keys(
        key_local, value_local, backward_visit, ((empty_query, empty_query), empty_keys, empty_keys)
    )
    key_own, value_own = (
        lax.psum_scatter(
            key_total.astype(jnp.bfloat16), "ctx", scatter_dimension=0, tiled=True
        ).astype(jnp.float32),
        lax.psum_scatter(
            value_total.astype(jnp.bfloat16), "ctx", scatter_dimension=0, tiled=True
        ).astype(jnp.float32),
    )
    query_grad = jnp.transpose(jnp.concatenate(query_accs, axis=2), (2, 0, 1, 3)).reshape(
        shard_rows, query_width
    )
    grads_packed = jnp.concatenate(
        [
            query_grad.astype(jnp.bfloat16),
            key_own.astype(jnp.bfloat16),
            value_own.astype(jnp.bfloat16),
        ],
        axis=1,
    )
    query_gradient = grads_packed[:, :query_width]
    key_gradient = grads_packed[:, query_width : query_width + kv_width]
    value_gradient = grads_packed[:, query_width + kv_width :]
    return (
        layer_out[None],
        residual_gradient[None],
        query_gradient[None],
        key_gradient[None],
        value_gradient[None],
        route_gradient[None],
    )


def solution(mesh):
    in_specs = (
        P("exp", "ctx", None),
        P("exp", "ctx", None),
        P("exp", "ctx", None),
        P("exp", "ctx", None),
        P(),
        P("exp", "ctx", None),
        P("exp", "ctx", None),
        P(("ctx", "exp"), None, None),
        P(("ctx", "exp"), None, None),
        P(("ctx", "exp"), None, None),
        P("exp", "ctx", None),
    )
    out_specs = (
        P("exp", "ctx", None),
        P("exp", "ctx", None),
        P("exp", "ctx", None),
        P("exp", "ctx", None),
        P("exp", "ctx", None),
        P("exp", "ctx", None),
    )
    return jax.shard_map(
        per_device, mesh=mesh, in_specs=in_specs, out_specs=out_specs, check_vma=False
    )
```

profile of v0, /device:TPU:0, one launch (start us, length us, event | category | flops | bytes accessed | tf_op | source)
XLA Modules:
  0.0 1245.4 jit_solution(13929531508248828289)
XLA Ops:
  7.2 1.7 copy.64
  9.0 1.6 copy.65
  17.2 2.6 convert_bitcast_fusion
  19.8 10.2 scatter_custom_fusion.1
  29.9 8.1 reshape.375
  38.1 11.7 all-to-all-start.2
  53.6 173.6 %all-gather.5.cloned.1.call-done = bf16[1,4096,256]{1,2,0:T(8,128)(2,1)} async-done(((bf16[1,128,256]{1,2,0:T(8,128)(2,1)}), bf16[1,4096,256]{1,2,0:T(8,128)(2,1)}) %all-gather.5.cloned.1.call-update) | async-done | bytes 2097168 | tf_op jit(solution)/shard_map/all_gather | solution.py:23
  227.2 126.3 %all-gather.7.cloned.1.call-done = bf16[1,4096,256]{1,2,0:T(8,128)(2,1)} async-done(((bf16[1,128,256]{1,2,0:T(8,128)(2,1)}), bf16[1,4096,256]{1,2,0:T(8,128)(2,1)}) %all-gather.7.cloned.1.call-update) | async-done | bytes 2097168 | tf_op jit(solution)/shard_map/all_gather | solution.py:24
  353.5 28.2 %conditional.5 = (f32[2,8,64]{2,1,0:T(8,128)}, f32[2,8,64]{2,1,0:T(8,128)}, f32[2,8,64,128]{3,2,1,0:T(8,128)S(1)}, f32[2,8,64]{2,1,0:T(8,128)S(1)}) conditional(s32[]{:T(128)} %convert_element_type.216, () %tuple.46, (s32[4096]{0:T(1024)S(1)}, s32[64]{0:T(128)S(1)}, bf16[4096,2,128]{0,2,1:T(8,128)(2,1)}, bf16[64,2,8,128]{3,2,1,0:T(8,128)(2,1)S(1)}, ...), branch_computations={%region_6.7_spmd, %region_7.10_spmd} | conditional | flops 2202270720 | bytes 56410400 | solution.py:137
  353.9 9.0 fusion.13
  363.5 8.2 fusion.16
  371.8 9.2 fusion.15
  382.5 29.6 %conditional.4 = (f32[2,8,64]{2,1,0:T(8,128)}, f32[2,8,64]{2,1,0:T(8,128)}, f32[2,8,64,128]{3,2,1,0:T(8,128)S(1)}, f32[2,8,64]{2,1,0:T(8,128)S(1)}) conditional(s32[]{:T(128)} %convert_element_type.215, () %tuple.44, (s32[4096]{0:T(1024)S(1)}, s32[64]{0:T(128)S(1)}, bf16[4096,2,128]{0,2,1:T(8,128)(2,1)}, bf16[64,2,8,128]{3,2,1,0:T(8,128)(2,1)}, ...), branch_computations={%region_1.0_spmd, %region_2.5_spmd} | conditional | flops 2202270720 | bytes 56410400 | solution.py:137
  382.7 10.2 fusion
  393.5 8.2 fusion.3
  401.8 9.2 fusion.2
  412.1 1.5 broadcast_divide_fusion
  417.7 9.9 scatter_custom_fusion
  427.6 8.1 reshape.371
  435.7 8.8 all-to-all-start
  444.5 8.4 reshape.376
  453.0 8.9 fusion.95
  461.9 90.1 %all-to-all-done = bf16[128,9,2048]{2,1,0:T(8,128)(2,1)} async-done(((bf16[128,9,2048]{2,1,0:T(8,128)(2,1)}), bf16[128,9,2048]{2,1,0:T(8,128)(2,1)}, u32[]{:S(2)}, u32[]{:S(2)}) %all-to-all-start) | async-done | bytes 4718624 | tf_op jit(solution)/shard_map/all_to_all | solution.py:31
  552.0 8.5 reshape.372
  560.5 5.9 fusion.103
  566.4 3.9 fusion.99
  570.3 1.7 copy-done.38
  572.1 8.3 fusion.101
  580.3 8.3 add_convert_fusion
  588.6 8.1 reshape.377
  596.7 11.1 all-to-all-start.3
  608.0 1.2 copy.138
  609.2 1.2 copy.136
  610.4 106.7 %all-to-all-done.3 = bf16[128,9,2048]{2,1,0:T(8,128)(2,1)} async-done(((bf16[128,9,2048]{2,1,0:T(8,128)(2,1)}), bf16[128,9,2048]{2,1,0:T(8,128)(2,1)}, u32[]{:S(2)}, u32[]{:S(2)}) %all-to-all-start.3) | async-done | bytes 4718624 | tf_op jit(solution)/shard_map/all_to_all | solution.py:35
  717.1 8.4 reshape.378
  725.5 11.8 gather_fusion.1
  737.3 5.2 convert_reduce_fusion
  743.6 1.2 fusion.128
  744.8 39.8 %conditional.6 = (f32[4096,2,128]{2,0,1:T(8,128)}, f32[4096,2,128]{2,0,1:T(8,128)}, bf16[2,8,64,128]{3,2,1,0:T(8,128)(2,1)S(1)}) conditional(s32[]{:T(128)} %convert_element_type.215, () %tuple.48, (s32[4096]{0:T(1024)S(1)}, s32[64]{0:T(128)S(1)}, bf16[4096,2,128]{0,2,1:T(8,128)(2,1)S(1)}, bf16[64,2,8,128]{3,2,1,0:T(8,128)(2,1)S(1)}, ...), branch_computations={%region_20.21_spmd, %region_21.22_spmd} | conditional | flops 5412226048 | bytes 95461712 | solution.py:267
  746.3 8.1 fusion.42
  754.4 12.9 %fusion.34 = f32[4096,2,128]{2,0,1:T(8,128)} fusion(f32[2,4096,64,8]{1,2,3,0:T(8,128)} %fusion.42, f32[2,8,64]{2,1,0:T(8,128)S(1)} %add.75, pred[64,4096]{1,0:T(8,128)(4,1)S(1)} %broadcast_compare_fusion.2, bf16[64,2,8,128]{3,2,1,0:T(8,128)(2,1)S(1)} %bitcast.303), kind=kOutput, calls=%fused_computation.45 | convolution fusion | flops 1090519040 | bytes 21499904 | tf_op jit(solution)/shard_map/cond/branch_1_fun/kgij,ikgd->jkd/dot_general | solution.py:76
  767.3 9.5 fusion.27
  776.8 2.3 fusion.47
  779.1 5.3 fusion.38
  785.4 40.5 %conditional.7 = (f32[4096,2,128]{2,0,1:T(8,128)}, f32[4096,2,128]{2,0,1:T(8,128)}, bf16[2,8,64,128]{3,2,1,0:T(8,128)(2,1)S(1)}) conditional(s32[]{:T(128)} %convert_element_type.216, () %tuple.50, (s32[4096]{0:T(1024)S(1)}, s32[64]{0:T(128)S(1)}, bf16[4096,2,128]{0,2,1:T(8,128)(2,1)S(1)}, bf16[64,2,8,128]{3,2,1,0:T(8,128)(2,1)S(1)}, ...), branch_computations={%region_22.23_spmd, %region_23.24_spmd} | conditional | flops 5412226048 | bytes 93372696 | solution.py:267
  787.4 8.1 fusion.72
  795.4 12.9 %fusion.64 = f32[4096,2,128]{2,0,1:T(8,128)} fusion(f32[2,4096,64,8]{1,2,3,0:T(8,128)} %fusion.72, f32[2,8,64]{2,1,0:T(8,128)S(1)} %add.76, pred[64,4096]{1,0:T(8,128)(4,1)S(1)} %broadcast_compare_fusion.3, bf16[64,2,8,128]{3,2,1,0:T(8,128)(2,1)S(1)} %bitcast.301), kind=kOutput, calls=%fused_computation.73 | convolution fusion | flops 1090519040 | bytes 21499904 | tf_op jit(solution)/shard_map/cond/branch_1_fun/kgij,ikgd->jkd/dot_general | solution.py:76
  808.3 9.6 fusion.57
  817.9 2.3 fusion.77
  820.2 5.3 fusion.68
  825.9 5.3 copy_bitcast_fusion.1
  831.2 10.0 convolution_convert_fusion
  841.2 8.1 reshape.373
  849.4 10.3 all-to-all-start.1
  859.7 5.3 copy_bitcast_fusion
  865.2 1.1 reshape.379
  866.3 100.4 %all-to-all-done.1 = bf16[128,9,2048]{2,1,0:T(8,128)(2,1)} async-done(((bf16[128,9,2048]{2,1,0:T(8,128)(2,1)}), bf16[128,9,2048]{2,1,0:T(8,128)(2,1)}, u32[]{:S(2)}, u32[]{:S(2)}) %all-to-all-start.1) | async-done | bytes 4718624 | tf_op jit(solution)/shard_map/all_to_all | solution.py:35
  966.8 8.4 reshape.374
  975.2 11.8 gather_fusion
  987.0 6.1 fusion.87
  996.2 2.1 convert_element_type.257
  998.2 3.6 fusion.119
  1001.8 73.6 %reduce-scatter.3.cloned.1.call-done = bf16[128,256]{1,0:T(8,128)(2,1)} async-done(((bf16[4096,256]{1,0:T(8,128)(2,1)}), bf16[128,256]{1,0:T(8,128)(2,1)}) %reduce-scatter.3.cloned.1.call-update) | async-done | bytes 65552 | tf_op jit(solution)/shard_map/reduce_scatter | solution.py:297
  1075.4 162.9 %reduce-scatter.5.cloned.1.call-done = bf16[128,256]{1,0:T(8,128)(2,1)} async-done(((bf16[4096,256]{1,0:T(8,128)(2,1)}), bf16[128,256]{1,0:T(8,128)(2,1)}) %reduce-scatter.5.cloned.1.call-update) | async-done | bytes 65552 | tf_op jit(solution)/shard_map/reduce_scatter | solution.py:300
  (148 shorter events, 25.2 us)
Async XLA Ops:
  7.2 553.3 %copy-start = (bf16[1,2048,768]{2,1,0:T(8,128)(2,1)S(1)}, bf16[1,2048,768]{2,1,0:T(8,128)(2,1)}, u32[]{:S(2)}) copy-start(bf16[1,2048,768]{2,1,0:T(8,128)(2,1)} %param.26) | copy-start | bytes 9437188
  7.2 220.0 %all-gather.5.cloned.1.call-start = ((), (), s32[]{:S(2)}) async-start(), calls=%async_computation.8 | async-start | bytes 2162688 | tf_op jit(solution)/shard_map/all_gather | solution.py:23
  9.0 344.5 %all-gather.7.cloned.1.call-start = ((), (), s32[]{:S(2)}) async-start(), calls=%async_computation.9 | async-start | bytes 2162688 | tf_op jit(solution)/shard_map/all_gather | solution.py:24
  13.1 16.9 %copy-start.25 = (f32[1,128,8]{2,1,0:T(8,128)}, f32[1,128,8]{2,1,0:T(8,128)S(1)}, u32[]{:S(2)}) copy-start(f32[1,128,8]{2,1,0:T(8,128)S(1)} %copy.73) | copy-start | bytes 12292
  13.8 0.6 copy-start.31
  14.8 0.8 copy-start.22
  38.1 397.6 %all-to-all-start.2 = ((bf16[128,9,2048]{2,1,0:T(8,128)(2,1)}), bf16[128,9,2048]{2,1,0:T(8,128)(2,1)}, u32[]{:S(2)}, u32[]{:S(2)}) async-start(bf16[128,9,2048]{2,1,0:T(8,128)(2,1)} %reshape.375), calls=%async_computation.2 | async-start | bytes 16777216 | tf_op jit(solution)/shard_map/all_to_all | solution.py:31
  381.7 0.8 copy-start.23
  412.1 3.3 copy-start.9
  412.1 4.6 copy-start.30
  413.6 0.7 copy-start.18
  413.6 0.8 copy-start.20
  414.4 1.0 copy-start.4
  415.9 0.8 copy-start.6
  416.0 327.6 %copy-start.33 = (f32[128]{0:T(128)}, f32[128]{0:T(128)S(1)}, u32[]{:S(2)}) copy-start(f32[128]{0:T(128)S(1)} %get-tuple-element.208) | copy-start | bytes 1540
  435.7 116.3 %all-to-all-start = ((bf16[128,9,2048]{2,1,0:T(8,128)(2,1)}), bf16[128,9,2048]{2,1,0:T(8,128)(2,1)}, u32[]{:S(2)}, u32[]{:S(2)}) async-start(bf16[128,9,2048]{2,1,0:T(8,128)(2,1)} %reshape.371), calls=%async_computation | async-start | bytes 16777216 | tf_op jit(solution)/shard_map/all_to_all | solution.py:31
  560.5 5.9 copy-start.8
  560.5 5.9 copy-start.35
  566.4 13.9 %copy-start.36 = (f32[1152,768]{1,0:T(8,128)}, f32[1152,768]{1,0:T(8,128)S(1)}, u32[]{:S(2)}) copy-start(f32[1152,768]{1,0:T(8,128)S(1)} %fusion.103) | copy-start | bytes 10616836
  566.4 5.6 copy-start.37
  570.3 1.8 copy-start.38
  596.7 11.2 copy-start.10
  596.7 12.4 copy-start.14
  596.7 120.4 %all-to-all-start.3 = ((bf16[128,9,2048]{2,1,0:T(8,128)(2,1)}), bf16[128,9,2048]{2,1,0:T(8,128)(2,1)}, u32[]{:S(2)}, u32[]{:S(2)}) async-start(bf16[128,9,2048]{2,1,0:T(8,128)(2,1)} %reshape.377), calls=%async_computation.3 | async-start | bytes 16777216 | tf_op jit(solution)/shard_map/all_to_all | solution.py:35
  607.8 467.6 %reduce-scatter.3.cloned.1.call-start = ((), (), s32[]{:S(2)}) async-start(), calls=%async_computation.6 | async-start | bytes 2162688 | tf_op jit(solution)/shard_map/reduce_scatter | solution.py:297
  737.3 5.2 copy-start.7
  737.3 5.7 copy-start.11
  737.3 6.3 copy-start.12
  737.3 6.3 copy-start.13
  737.3 6.3 copy-start.19
  737.3 6.3 copy-start.21
  742.5 2.3 copy-start.3
  742.5 2.3 copy-start.2
  742.5 2.3 copy-start.15
  742.8 2.0 copy-start.34
  743.6 1.3 copy-start.24
  745.3 1.0 copy-start.16
  776.8 2.4 copy-start.17
  784.6 0.7 copy-start.27
  825.9 5.3 copy-start.29
  849.4 117.4 %all-to-all-start.1 = ((bf16[128,9,2048]{2,1,0:T(8,128)(2,1)}), bf16[128,9,2048]{2,1,0:T(8,128)(2,1)}, u32[]{:S(2)}, u32[]{:S(2)}) async-start(bf16[128,9,2048]{2,1,0:T(8,128)(2,1)} %reshape.373), calls=%async_computation.1 | async-start | bytes 16777216 | tf_op jit(solution)/shard_map/all_to_all | solution.py:35
  859.6 378.7 %reduce-scatter.5.cloned.1.call-start = ((), (), s32[]{:S(2)}) async-start(), calls=%async_computation.7 | async-start | bytes 2162688 | tf_op jit(solution)/shard_map/reduce_scatter | solution.py:300
  859.7 5.4 copy-start.26
  859.7 5.4 copy-start.32
  859.7 5.5 copy-start.5
  987.0 7.0 copy-start.28
  987.0 251.3 %copy-start.1 = (bf16[1,2048,768]{2,1,0:T(8,128)(2,1)S(1)}, bf16[1,2048,768]{2,1,0:T(8,128)(2,1)}, u32[]{:S(2)}) copy-start(bf16[1,2048,768]{2,1,0:T(8,128)(2,1)} %param.26) | copy-start | bytes 9437188
Sparse Core Ops, SparseCore 0:
  10.2 217.0 all-gather.4
  229.4 124.1 all-gather.6
  831.3 244.0 reduce-scatter.2
  1078.3 159.9 reduce-scatter.4
where the time goes:
time: 1250 us
  waiting for transfers between devices  834 us (67%)
  matrix products  157 us (13%)
  local copies, waits for them, and re-layouts  124 us (10%)
  other arithmetic  70.5 us (6%)
  starting transfers between devices  42 us (3%)
  between operations  16.2 us (1%)
    all_to_all x2, waiting for transfers between devices, from_experts(): lax.all_to_all(rows_back, ('ctx', 'exp'), split_axis=0, concat_axis=0, ti...  207 us
    all_gather x1, waiting for transfers between devices, over_keys(): lax.all_gather(key_local, 'ctx', axis=0, tiled=True)  174 us
    reduce_scatter x1, waiting for transfers between devices, per_device(): lax.psum_scatter(value_total.astype(jnp.bfloat16), 'ctx', scatter_dimensi...  163 us
    all_gather x1, waiting for transfers between devices, over_keys(): lax.all_gather(value_local, 'ctx', axis=0, tiled=True)  126 us
    all_to_all x2, waiting for transfers between devices, to_experts(): lax.all_to_all(rows_out, ('ctx', 'exp'), split_axis=0, concat_axis=0, til...  90.1 us
    reduce_scatter x1, waiting for transfers between devices, per_device(): lax.psum_scatter(key_total.astype(jnp.bfloat16), 'ctx', scatter_dimension...  73.6 us
    dot_general x2, matrix products, backward_tile(): jnp.einsum('kgij,ikgd->jkd', weights.astype(jnp.bfloat16), grad_half, pre...  25.8 us
  transfers between devices with their start and end apart: 8, of which 7 were waited for; matrix products, arithmetic and copies ran while one was open for 15% of the time, Pallas kernels for 0%

commit v1 on v0

--- a/solution.py
+++ b/solution.py
@@ -21,7 +21,9 @@
         start_state,
         (
             lax.all_gather(key_local, "ctx", axis=0, tiled=True),
-            lax.all_gather(value_local, "ctx", axis=0, tiled=True),
+            jnp.concatenate(
+                lax.all_to_all(jnp.stack([value_local] * lax.axis_size("ctx")), "ctx", 0, 0), axis=0
+            ),
         ),
         jnp.int32(0),
     )

time: 1250 us -> 1150 us (0.920)
  waiting for transfers between devices: 834 us -> 716 us
    all_gather x1 -> x0, waiting for transfers between devices: 126 us -> none  [over_keys(): lax.all_gather(value_local, 'ctx', axis=0, tiled=True)]
  transfers between devices with their start and end apart: 8 -> 8, of which waited for: 7 -> 7; matrix products, arithmetic and copies ran while one was open for 15% -> 17% of each run, Pallas kernels for 0% -> 0%
where the time goes in v1:
time: 1150 us; the launch traced here: 1140 us
  waiting for transfers between devices  716 us (62%)
  matrix products  157 us (14%)
  local copies, waits for them, and re-layouts  131 us (11%)
  other arithmetic  69.1 us (6%)
  starting transfers between devices  49.2 us (4%)
  between operations  16.2 us (1%)
    all_to_all x2, waiting for transfers between devices, from_experts(): lax.all_to_all(rows_back, ('ctx', 'exp'), split_axis=0, concat_axis=0, ti...  208 us
    all_gather x1, waiting for transfers between devices, over_keys(): lax.all_gather(key_local, 'ctx', axis=0, tiled=True)  175 us
    reduce_scatter x1, waiting for transfers between devices, per_device(): lax.psum_scatter(value_total.astype(jnp.bfloat16), 'ctx', scatter_dimensi...  166 us
    all_to_all x2, waiting for transfers between devices, to_experts(): lax.all_to_all(rows_out, ('ctx', 'exp'), split_axis=0, concat_axis=0, til...  90 us
    reduce_scatter x1, waiting for transfers between devices, per_device(): lax.psum_scatter(key_total.astype(jnp.bfloat16), 'ctx', scatter_dimension...  74.3 us
    dot_general x2, matrix products, backward_tile(): jnp.einsum('kgij,ikgd->jkd', weights.astype(jnp.bfloat16), grad_half, pre...  25.8 us
  transfers between devices with their start and end apart: 8, of which 7 were waited for; matrix products, arithmetic and copies ran while one was open for 17% of the time, Pallas kernels for 0%

profile of v1, /device:TPU:0, one launch (start us, length us, event | category | flops | bytes accessed | tf_op | source)
XLA Modules:
  0.0 1140.9 jit_solution(18320557088927829104)
XLA Ops:
  8.3 1.9 stack.4
  10.2 9.4 all-to-all-start
  24.2 2.6 convert_bitcast_fusion
  26.8 10.1 scatter_custom_fusion.1
  36.9 8.1 reshape.371
  45.1 3.0 all-to-all-done
  48.0 10.5 all-to-all-start.3
  62.4 4.3 copy.66
  66.7 4.2 reshape_reshape.4
  70.8 175.3 %all-gather.3.cloned.1.call-done = bf16[1,4096,256]{1,2,0:T(8,128)(2,1)} async-done(((bf16[1,128,256]{1,2,0:T(8,128)(2,1)}), bf16[1,4096,256]{1,2,0:T(8,128)(2,1)}) %all-gather.3.cloned.1.call-update) | async-done | bytes 2097168 | tf_op jit(solution)/shard_map/all_gather | solution.py:23
  246.2 29.4 %conditional.4 = (f32[2,8,64]{2,1,0:T(8,128)}, f32[2,8,64]{2,1,0:T(8,128)}, f32[2,8,64,128]{3,2,1,0:T(8,128)S(1)}, f32[2,8,64]{2,1,0:T(8,128)S(1)}) conditional(s32[]{:T(128)} %convert_element_type.215, () %tuple.44, (s32[4096]{0:T(1024)S(1)}, s32[64]{0:T(128)S(1)}, bf16[4096,2,128]{0,2,1:T(8,128)(2,1)}, bf16[64,2,8,128]{3,2,1,0:T(8,128)(2,1)}, ...), branch_computations={%region_1.0_spmd, %region_2.5_spmd} | conditional | flops 2202270720 | bytes 56410400 | solution.py:139
  246.6 10.2 fusion
  257.4 8.2 fusion.3
  265.6 9.2 fusion.2
  276.3 28.4 %conditional.5 = (f32[2,8,64]{2,1,0:T(8,128)}, f32[2,8,64]{2,1,0:T(8,128)}, f32[2,8,64,128]{3,2,1,0:T(8,128)S(1)}, f32[2,8,64]{2,1,0:T(8,128)S(1)}) conditional(s32[]{:T(128)} %convert_element_type.216, () %tuple.46, (s32[4096]{0:T(1024)S(1)}, s32[64]{0:T(128)S(1)}, bf16[4096,2,128]{0,2,1:T(8,128)(2,1)}, bf16[64,2,8,128]{3,2,1,0:T(8,128)(2,1)S(1)}, ...), branch_computations={%region_6.7_spmd, %region_7.10_spmd} | conditional | flops 2202270720 | bytes 56410400 | solution.py:139
  276.6 9.0 fusion.13
  286.2 8.2 fusion.16
  294.4 9.2 fusion.15
  304.7 1.4 broadcast_divide_fusion
  310.3 9.9 scatter_custom_fusion
  320.2 8.1 reshape.367
  328.3 7.8 all-to-all-start.1
  336.1 8.4 reshape.372
  344.5 9.0 fusion.95
  353.5 90.0 %all-to-all-done.1 = bf16[128,9,2048]{2,1,0:T(8,128)(2,1)} async-done(((bf16[128,9,2048]{2,1,0:T(8,128)(2,1)}), bf16[128,9,2048]{2,1,0:T(8,128)(2,1)}, u32[]{:S(2)}, u32[]{:S(2)}) %all-to-all-start.1) | async-done | bytes 4718624 | tf_op jit(solution)/shard_map/all_to_all | solution.py:33
  443.5 8.5 reshape.368
  452.0 5.8 fusion.103
  457.9 3.9 fusion.99
  461.8 1.7 copy-done.41
  463.6 8.2 fusion.101
  471.8 8.3 add_convert_fusion
  480.1 8.1 reshape.373
  488.2 11.1 all-to-all-start.4
  499.5 1.2 copy.139
  500.7 1.2 copy.137
  501.9 106.7 %all-to-all-done.4 = bf16[128,9,2048]{2,1,0:T(8,128)(2,1)} async-done(((bf16[128,9,2048]{2,1,0:T(8,128)(2,1)}), bf16[128,9,2048]{2,1,0:T(8,128)(2,1)}, u32[]{:S(2)}, u32[]{:S(2)}) %all-to-all-start.4) | async-done | bytes 4718624 | tf_op jit(solution)/shard_map/all_to_all | solution.py:37
  608.6 8.4 reshape.374
  617.0 11.8 %gather_fusion.1 = bf16[1024,2048]{1,0:T(8,128)(2,1)} fusion(bf16[1152,2048]{1,0:T(8,128)(2,1)} %reshape.374, s32[1024]{0:T(1024)S(1)} %broadcast_clamp_fusion), kind=kCustom, calls=%fused_computation.1 | custom fusion | bytes 8392704 | tf_op jit(solution)/shard_map/gather | solution.py:237
  628.8 5.2 convert_reduce_fusion
  636.3 39.8 %conditional.6 = (f32[4096,2,128]{2,0,1:T(8,128)}, f32[4096,2,128]{2,0,1:T(8,128)}, bf16[2,8,64,128]{3,2,1,0:T(8,128)(2,1)S(1)}) conditional(s32[]{:T(128)} %convert_element_type.215, () %tuple.48, (s32[4096]{0:T(1024)S(1)}, s32[64]{0:T(128)S(1)}, bf16[4096,2,128]{0,2,1:T(8,128)(2,1)S(1)}, bf16[64,2,8,128]{3,2,1,0:T(8,128)(2,1)S(1)}, ...), branch_computations={%region_20.21_spmd, %region_21.22_spmd} | conditional | flops 5412226048 | bytes 95461712 | solution.py:269
  637.8 8.1 fusion.42
  645.8 12.9 %fusion.34 = f32[4096,2,128]{2,0,1:T(8,128)} fusion(f32[2,4096,64,8]{1,2,3,0:T(8,128)} %fusion.42, f32[2,8,64]{2,1,0:T(8,128)S(1)} %add.75, pred[64,4096]{1,0:T(8,128)(4,1)S(1)} %broadcast_compare_fusion.2, bf16[64,2,8,128]{3,2,1,0:T(8,128)(2,1)S(1)} %bitcast.305), kind=kOutput, calls=%fused_computation.45 | convolution fusion | flops 1090519040 | bytes 21499904 | tf_op jit(solution)/shard_map/cond/branch_1_fun/kgij,ikgd->jkd/dot_general | solution.py:78
  658.7 9.5 fusion.27
  668.2 2.3 fusion.47
  670.6 5.3 fusion.38
  676.8 40.5 %conditional.7 = (f32[4096,2,128]{2,0,1:T(8,128)}, f32[4096,2,128]{2,0,1:T(8,128)}, bf16[2,8,64,128]{3,2,1,0:T(8,128)(2,1)S(1)}) conditional(s32[]{:T(128)} %convert_element_type.216, () %tuple.50, (s32[4096]{0:T(1024)S(1)}, s32[64]{0:T(128)S(1)}, bf16[4096,2,128]{0,2,1:T(8,128)(2,1)S(1)}, bf16[64,2,8,128]{3,2,1,0:T(8,128)(2,1)S(1)}, ...), branch_computations={%region_22.23_spmd, %region_23.24_spmd} | conditional | flops 5412226048 | bytes 93372696 | solution.py:269
  678.8 8.1 fusion.72
  686.9 12.9 %fusion.64 = f32[4096,2,128]{2,0,1:T(8,128)} fusion(f32[2,4096,64,8]{1,2,3,0:T(8,128)} %fusion.72, f32[2,8,64]{2,1,0:T(8,128)S(1)} %add.76, pred[64,4096]{1,0:T(8,128)(4,1)S(1)} %broadcast_compare_fusion.3, bf16[64,2,8,128]{3,2,1,0:T(8,128)(2,1)S(1)} %bitcast.303), kind=kOutput, calls=%fused_computation.73 | convolution fusion | flops 1090519040 | bytes 21499904 | tf_op jit(solution)/shard_map/cond/branch_1_fun/kgij,ikgd->jkd/dot_general | solution.py:78
  699.8 9.6 fusion.57
  709.4 2.3 fusion.77
  711.7 5.3 fusion.68
  717.3 5.3 copy_bitcast_fusion.1
  722.7 10.0 convolution_convert_fusion
  732.7 8.1 reshape.369
  740.8 10.3 all-to-all-start.2
  751.1 5.3 copy_bitcast_fusion
  757.8 100.9 %all-to-all-done.2 = bf16[128,9,2048]{2,1,0:T(8,128)(2,1)} async-done(((bf16[128,9,2048]{2,1,0:T(8,128)(2,1)}), bf16[128,9,2048]{2,1,0:T(8,128)(2,1)}, u32[]{:S(2)}, u32[]{:S(2)}) %all-to-all-start.2) | async-done | bytes 4718624 | tf_op jit(solution)/shard_map/all_to_all | solution.py:37
  858.7 8.4 reshape.370
  867.1 11.8 %gather_fusion = bf16[1024,2048]{1,0:T(8,128)(2,1)} fusion(bf16[1152,2048]{1,0:T(8,128)(2,1)} %reshape.370, s32[1024]{0:T(1024)S(1)} %broadcast_clamp_fusion), kind=kCustom, calls=%fused_computation | custom fusion | bytes 8392704 | tf_op jit(solution)/shard_map/gather | solution.py:208
  878.8 6.1 fusion.87
  888.0 2.1 convert_element_type.257
  890.1 3.6 fusion.119
  893.7 74.3 %reduce-scatter.3.cloned.1.call-done = bf16[128,256]{1,0:T(8,128)(2,1)} async-done(((bf16[4096,256]{1,0:T(8,128)(2,1)}), bf16[128,256]{1,0:T(8,128)(2,1)}) %reduce-scatter.3.cloned.1.call-update) | async-done | bytes 65552 | tf_op jit(solution)/shard_map/reduce_scatter | solution.py:299
  968.0 165.9 %reduce-scatter.5.cloned.1.call-done = bf16[128,256]{1,0:T(8,128)(2,1)} async-done(((bf16[4096,256]{1,0:T(8,128)(2,1)}), bf16[128,256]{1,0:T(8,128)(2,1)}) %reduce-scatter.5.cloned.1.call-update) | async-done | bytes 65552 | tf_op jit(solution)/shard_map/reduce_scatter | solution.py:302
  (156 shorter events, 26.5 us)
Async XLA Ops:
  7.2 444.9 %copy-start = (bf16[1,2048,768]{2,1,0:T(8,128)(2,1)S(1)}, bf16[1,2048,768]{2,1,0:T(8,128)(2,1)}, u32[]{:S(2)}) copy-start(bf16[1,2048,768]{2,1,0:T(8,128)(2,1)} %param.26) | copy-start | bytes 9437188
  7.2 12.5 %copy-start.31 = (bf16[1,128,256]{2,1,0:T(8,128)(2,1)S(1)}, bf16[1,128,256]{2,1,0:T(8,128)(2,1)}, u32[]{:S(2)}) copy-start(bf16[1,128,256]{2,1,0:T(8,128)(2,1)} %param.21) | copy-start | bytes 196612
  7.2 13.2 %copy-start.33 = (s32[1,128,8]{1,2,0:T(8,128)S(1)}, s32[1,128,8]{1,2,0:T(8,128)}, u32[]{:S(2)}) copy-start(s32[1,128,8]{1,2,0:T(8,128)} %param.24) | copy-start | bytes 12292
  7.2 13.5 %copy-start.32 = (f32[1,128,8]{1,2,0:T(8,128)S(1)}, f32[1,128,8]{1,2,0:T(8,128)}, u32[]{:S(2)}) copy-start(f32[1,128,8]{1,2,0:T(8,128)} %param.25) | copy-start | bytes 12292
  10.2 37.8 %all-to-all-start = ((bf16[32,128,256]{1,2,0:T(8,128)(2,1)}), bf16[32,128,256]{1,2,0:T(8,128)(2,1)}, u32[]{:S(2)}, u32[]{:S(2)}) async-start(bf16[32,128,256]{1,2,0:T(8,128)(2,1)} %stack.4), calls=%async_computation | async-start | bytes 4194304 | tf_op jit(solution)/shard_map/all_to_all | solution.py:25
  19.6 226.6 %all-gather.3.cloned.1.call-start = ((), (), s32[]{:S(2)}) async-start(), calls=%async_computation.9 | async-start | bytes 2162688 | tf_op jit(solution)/shard_map/all_gather | solution.py:23
  20.8 16.1 %copy-start.25 = (f32[1,128,8]{2,1,0:T(8,128)}, f32[1,128,8]{2,1,0:T(8,128)S(1)}, u32[]{:S(2)}) copy-start(f32[1,128,8]{2,1,0:T(8,128)S(1)} %copy.74) | copy-start | bytes 12292
  20.8 0.5 copy-start.34
  21.7 0.8 copy-start.22
  48.0 280.3 %all-to-all-start.3 = ((bf16[128,9,2048]{2,1,0:T(8,128)(2,1)}), bf16[128,9,2048]{2,1,0:T(8,128)(2,1)}, u32[]{:S(2)}, u32[]{:S(2)}) async-start(bf16[128,9,2048]{2,1,0:T(8,128)(2,1)} %reshape.371), calls=%async_computation.3 | async-start | bytes 16777216 | tf_op jit(solution)/shard_map/all_to_all | solution.py:33
  275.5 0.8 copy-start.23
  304.7 3.3 copy-start.9
  304.7 4.6 copy-start.30
  306.2 0.7 copy-start.18
  306.2 0.8 copy-start.20
  307.0 1.0 copy-start.4
  308.6 0.8 copy-start.6
  308.6 326.5 %copy-start.36 = (f32[128]{0:T(128)}, f32[128]{0:T(128)S(1)}, u32[]{:S(2)}) copy-start(f32[128]{0:T(128)S(1)} %get-tuple-element.208) | copy-start | bytes 1540
  328.3 115.2 %all-to-all-start.1 = ((bf16[128,9,2048]{2,1,0:T(8,128)(2,1)}), bf16[128,9,2048]{2,1,0:T(8,128)(2,1)}, u32[]{:S(2)}, u32[]{:S(2)}) async-start(bf16[128,9,2048]{2,1,0:T(8,128)(2,1)} %reshape.367), calls=%async_computation.1 | async-start | bytes 16777216 | tf_op jit(solution)/shard_map/all_to_all | solution.py:33
  452.0 5.9 copy-start.8
  452.0 5.9 copy-start.38
  457.9 13.9 %copy-start.39 = (f32[1152,768]{1,0:T(8,128)}, f32[1152,768]{1,0:T(8,128)S(1)}, u32[]{:S(2)}) copy-start(f32[1152,768]{1,0:T(8,128)S(1)} %fusion.103) | copy-start | bytes 10616836
  457.9 5.6 copy-start.40
  461.8 1.7 copy-start.41
  488.2 11.2 copy-start.10
  488.2 12.5 %copy-start.14 = (f32[16,8,16,128]{3,1,2,0:T(8,128)S(1)}, f32[16,8,16,128]{3,1,2,0:T(8,128)}, u32[]{:S(2)}) copy-start(f32[16,8,16,128]{3,1,2,0:T(8,128)} %get-tuple-element.204) | copy-start | bytes 3145732
  488.2 120.4 %all-to-all-start.4 = ((bf16[128,9,2048]{2,1,0:T(8,128)(2,1)}), bf16[128,9,2048]{2,1,0:T(8,128)(2,1)}, u32[]{:S(2)}, u32[]{:S(2)}) async-start(bf16[128,9,2048]{2,1,0:T(8,128)(2,1)} %reshape.373), calls=%async_computation.4 | async-start | bytes 16777216 | tf_op jit(solution)/shard_map/all_to_all | solution.py:37
  499.3 468.7 %reduce-scatter.3.cloned.1.call-start = ((), (), s32[]{:S(2)}) async-start(), calls=%async_computation.7 | async-start | bytes 2162688 | tf_op jit(solution)/shard_map/reduce_scatter | solution.py:299
  628.7 5.2 copy-start.7
  628.8 5.7 copy-start.11
  628.8 6.3 copy-start.12
  628.8 6.3 copy-start.13
  628.8 6.3 copy-start.19
  628.8 6.3 copy-start.21
  634.0 2.3 copy-start.3
  634.0 2.3 copy-start.2
  634.0 2.3 copy-start.15
  634.3 2.0 copy-start.37
  635.0 1.3 copy-start.24
  636.7 1.0 copy-start.16
  668.2 2.4 copy-start.17
  676.1 0.7 copy-start.27
  717.3 5.3 copy-start.29
  740.8 117.9 %all-to-all-start.2 = ((bf16[128,9,2048]{2,1,0:T(8,128)(2,1)}), bf16[128,9,2048]{2,1,0:T(8,128)(2,1)}, u32[]{:S(2)}, u32[]{:S(2)}) async-start(bf16[128,9,2048]{2,1,0:T(8,128)(2,1)} %reshape.369), calls=%async_computation.2 | async-start | bytes 16777216 | tf_op jit(solution)/shard_map/all_to_all | solution.py:37
  751.1 382.8 %reduce-scatter.5.cloned.1.call-start = ((), (), s32[]{:S(2)}) async-start(), calls=%async_computation.8 | async-start | bytes 2162688 | tf_op jit(solution)/shard_map/reduce_scatter | solution.py:302
  751.1 5.4 copy-start.26
  751.1 5.4 copy-start.35
  751.1 5.5 copy-start.5
  878.8 7.1 copy-start.28
  878.8 255.1 %copy-start.1 = (bf16[1,2048,768]{2,1,0:T(8,128)(2,1)S(1)}, bf16[1,2048,768]{2,1,0:T(8,128)(2,1)}, u32[]{:S(2)}) copy-start(bf16[1,2048,768]{2,1,0:T(8,128)(2,1)} %param.26) | copy-start | bytes 9437188
Sparse Core Ops, SparseCore 0:
  22.6 223.5 all-gather.2
  722.8 245.1 reduce-scatter.2
  971.1 162.7 reduce-scatter.4
